TPU v7x, 256 devices: a whole 4x4x8 slice. The times are simulated.
256 devices in a mesh: section: 16 (over z, core), inner: 16 (over y, x).
Axes of the slice: x: 4, y: 4, z: 8, core: 2. Of those that a mesh axis runs over, the one named last changes fastest.
Arguments:
- plant: float32 [256, 256], replicated, may hold values from 0 to 1
- actuation: float32 [256, 256], replicated, may hold values from -0.21875 to 0.21875
- state_weight: float32 [16, 256], P('section'), may hold values from 0.01 to 1
- input_weight: float32 [16, 256], P('section'), may hold values from 0.1 to 2
- state_grad: float32 [16, 256], P('section'), may hold values from -3 to 3
- input_grad: float32 [16, 256], P('section'), may hold values from -3 to 3
- defect: float32 [16, 256], P('section'), may hold values from -1.2 to 1.2
- terminal_hess: float32 [256, 256], replicated, as said below
- terminal_grad: float32 [256], replicated, may hold values from -6 to 6
Outputs:
- value_hess: float32 [16, 256, 256], P('section', 'inner')
- value_grad: float32 [16, 256], P('section', 'inner')
Inputs may be any that keep to these rules, and one draw needn't show every extreme that they name: `terminal_hess`: symmetric positive definite.
All inputs are finite; a program needn't handle non-finite values.
Results may differ from a plain program's by a relative error of at most 0.0002.
Values sent between devices are 32-bit elements; how exact they have to be, the bound alone decides.
No kernel may reach another device: no remote copies, remote signals or barrier semaphores. Data moves between devices by JAX's collectives and lax.ppermute only.
A program may use at most 128 MiB of HBM per device.

v0:
```python
import jax
import jax.numpy as jnp
from jax import lax
from jax.sharding import PartitionSpec as P

highest = lax.Precision.HIGHEST


def from_everyone(x, axis):
    copies = jnp.broadcast_to(x, (lax.axis_size(axis), *x.shape))
    return lax.all_to_all(copies, axis, split_axis=0, concat_axis=0, tiled=True)


def taken_together(x, axis):
    everything = from_everyone(x, axis)
    return jnp.sum(everything, axis=0)


def in_one_piece(arrays, axis, dim, along):
    ends, at = ([], 0)
    for a in arrays[:-1]:
        at += a.shape[along]
        ends.append(at)
    both = jnp.concatenate(arrays, axis=along)
    return tuple(jnp.split(lax.all_gather(both, axis, axis=dim, tiled=True), ends, axis=along))


def from_behind(value, axis, steps):
    count = lax.axis_size(axis)
    leading, last = (max(0, -steps), min(count, count - steps))
    return lax.ppermute(value, axis, [(source, source + steps) for source in range(leading, last)])


def matmul(first_mat, second_mat):
    return jnp.dot(first_mat, second_mat, precision=highest)


def lower_solve(factor, target):
    return jax.scipy.linalg.solve_triangular(factor, target, lower=True)


def upper_solve(factor, target):
    return jax.scipy.linalg.solve_triangular(factor, target, lower=True, trans=1)


def phase_element(plant, actuation, weights, inputs, gradient, input_gradient, defects):
    scaled = actuation / inputs[None, :]
    spread = matmul(scaled, actuation.T)
    drift_term = defects - matmul(scaled, input_gradient)
    return (plant, spread, jnp.diag(weights), drift_term, -gradient)


def fold_terminal(element, term_hess, term_linear):
    transition, spread, hessian_low, drift_term, linear_low = element
    identity = jnp.eye(term_hess.shape[0], dtype=term_hess.dtype)
    factor_j = jnp.linalg.cholesky(term_hess)
    coupled = matmul(spread, factor_j)
    factor_m = jnp.linalg.cholesky(identity + matmul(factor_j.T, coupled))
    pulled = matmul(lower_solve(factor_m, factor_j.T), transition)
    hessian = matmul(pulled.T, pulled) + hessian_low
    residue = term_linear - matmul(term_hess, drift_term)
    folded = upper_solve(factor_m, lower_solve(factor_m, matmul(coupled.T, residue)))
    linear = matmul(transition.T, residue - matmul(factor_j, folded)) + linear_low
    return (hessian, linear)


def combine(lower_part, upper_part, row_start, height):
    trans_low, spread_low, hess_low, drift_low, linear_low = lower_part
    trans_up, spread_up, hess_up, drift_up, linear_up = upper_part
    identity = jnp.eye(hess_up.shape[0], dtype=hess_up.dtype)
    factor_j = jnp.linalg.cholesky(hess_up)
    spread_local = lax.dynamic_slice_in_dim(spread_low, row_start, height, 0)
    factor_local = lax.dynamic_slice_in_dim(factor_j, row_start, height, 0)
    gram_share = matmul(factor_local.T, matmul(spread_local, factor_j))
    gram = taken_together(gram_share, "inner")
    factor_m = jnp.linalg.cholesky(identity + gram)
    up_rows = lax.dynamic_slice_in_dim(trans_up, row_start, height, 0)
    low_cols = lax.dynamic_slice_in_dim(trans_low, row_start, height, 1)
    up_spread = matmul(up_rows, spread_low)
    reflect_rows = lower_solve(factor_m, matmul(up_spread, factor_j).T).T
    pull_rows = lower_solve(factor_m, matmul(factor_j.T, low_cols)).T
    pull_all, reflect_all = in_one_piece((pull_rows, reflect_rows), "inner", 0, 1)
    hess_rows = matmul(pull_rows, pull_all.T) + hess_low
    trans_rows = matmul(up_rows, trans_low) - matmul(reflect_rows, pull_all.T)
    spread_rows = matmul(up_spread, trans_up.T) - matmul(reflect_rows, reflect_all.T) + spread_up
    pushed = drift_low + matmul(spread_low, linear_up)
    solved = upper_solve(factor_m, lower_solve(factor_m, matmul(factor_j.T, pushed)))
    pushed = pushed - matmul(spread_low, matmul(factor_j, solved))
    drift_new = matmul(trans_up, pushed) + drift_up
    residue = linear_up - matmul(hess_up, drift_low)
    mapped = matmul(factor_j.T, matmul(spread_low.T, residue))
    residue = residue - matmul(factor_j, upper_solve(factor_m, lower_solve(factor_m, mapped)))
    linear_new = matmul(trans_low.T, residue) + linear_low
    return (trans_rows, spread_rows, hess_rows, drift_new, linear_new)


def on_device(
    plant,
    actuation,
    state_weight,
    input_weight,
    state_grad,
    input_grad,
    defect,
    terminal_hess,
    terminal_grad,
):
    height = plant.shape[0] // lax.axis_size("inner")
    row_start = lax.axis_index("inner") * height
    phase_index = lax.axis_index("section")
    phase_count = lax.axis_size("section")
    at_top = phase_index == phase_count - 1
    below_top = phase_index == phase_count - 2
    identity = jnp.eye(plant.shape[0], dtype=plant.dtype)
    zero_mat = jnp.zeros_like(identity)
    own_phase = phase_element(
        plant, actuation, state_weight[0], input_weight[0], state_grad[0], input_grad[0], defect[0]
    )
    neighbour = from_behind(
        (state_weight, input_weight, state_grad, input_grad, defect), "section", -1
    )
    next_inputs = jnp.where(at_top, input_weight[0], neighbour[1][0])
    following = phase_element(
        plant,
        actuation,
        neighbour[0][0],
        next_inputs,
        neighbour[2][0],
        neighbour[3][0],
        neighbour[4][0],
    )
    source = tuple(
        (
            jnp.where(at_top, own_part, next_part)
            for own_part, next_part in zip(own_phase, following)
        )
    )

    def with_terminal():
        return fold_terminal(source, terminal_hess, -terminal_grad)

    def without_terminal():
        return (jnp.zeros_like(identity), jnp.zeros_like(terminal_grad))

    folded_hess, folded_linear = lax.cond(
        phase_index >= phase_count - 2, with_terminal, without_terminal
    )
    upper_part = (
        jnp.where(below_top, zero_mat, following[0]),
        lax.dynamic_slice_in_dim(
            jnp.where(below_top, zero_mat, following[1]), row_start, height, 0
        ),
        jnp.where(below_top, folded_hess, jnp.where(at_top, identity, following[2])),
        jnp.where(below_top, 0.0, following[3]),
        jnp.where(below_top, folded_linear, following[4]),
    )
    lower_part = (
        own_phase[0],
        own_phase[1],
        lax.dynamic_slice_in_dim(own_phase[2], row_start, height, 0),
        own_phase[3],
        own_phase[4],
    )
    joined = combine(lower_part, upper_part, row_start, height)
    top_rows = lax.dynamic_slice_in_dim(folded_hess, row_start, height, 0)
    zero_rows = jnp.zeros_like(top_rows)
    element = (
        jnp.where(at_top, zero_rows, joined[0]),
        jnp.where(at_top, zero_rows, joined[1]),
        jnp.where(at_top, top_rows, joined[2]),
        jnp.where(at_top, 0.0, joined[3]),
        jnp.where(at_top, folded_linear, joined[4]),
    )
    levels = phase_count.bit_length() - 1
    for exponent in range(1, levels):
        stride = 2**exponent
        trans_rows, spread_rows, hess_rows, drift_term, linear_term = element
        trans_full, spread_full, hess_full = in_one_piece(
            (trans_rows, spread_rows, hess_rows), "inner", 0, 1
        )
        received = from_behind(
            (trans_full, hess_full, spread_rows, drift_term, linear_term), "section", -stride
        )
        trans_up, hess_up, spread_up = (received[0], received[1], received[2])
        present = phase_index + stride < phase_count
        upper_part = (
            trans_up,
            spread_up,
            jnp.where(present, hess_up, identity),
            received[3],
            received[4],
        )
        lower_part = (trans_full, spread_full, hess_rows, drift_term, linear_term)
        joined = combine(lower_part, upper_part, row_start, height)
        element = tuple(
            (jnp.where(present, new_part, old_part) for new_part, old_part in zip(joined, element))
        )
    linear_rows = lax.dynamic_slice_in_dim(element[4], row_start, height, 0)
    return (element[2][None], -linear_rows[None])


def solution(mesh):
    in_specs = (
        P(),
        P(),
        P("section", None),
        P("section", None),
        P("section", None),
        P("section", None),
        P("section", None),
        P(),
        P(),
    )
    out_specs = (P("section", "inner", None), P("section", "inner"))
    return jax.shard_map(
        on_device, mesh=mesh, in_specs=in_specs, out_specs=out_specs, check_vma=False
    )
```

profile of v0, /device:TPU:22, one launch (start us, length us, event | category | flops | bytes accessed | tf_op | source)
XLA Modules:
  0.0 970.5 jit_solution(15490614688398979058)
XLA Ops:
  16.3 8.3 conditional.1
  24.9 11.7 %cholesky.534 = f32[128,128]{1,0:T(8,128)S(1)} custom-call(f32[128,128]{1,0:T(8,128)S(1)} %cholesky.808), custom_call_target="Cholesky" | custom-call | tf_op jit(solution)/shard_map/jit(cholesky)/cholesky | solution.py:71
  36.6 9.8 %custom-call.55 = f32[1,128,128]{1,2,0:T(8,128)S(1)} custom-call(f32[1,128,128]{2,1,0:T(8,128)S(1)} %get-tuple-element.391), custom_call_target="InvertDiagBlocksLowerTriangular" | custom-call | tf_op jit(solution)/shard_map/jit(cholesky)/cholesky | solution.py:71
  47.0 11.7 %cholesky.551 = f32[128,128]{1,0:T(8,128)S(1)} custom-call(f32[128,128]{1,0:T(8,128)S(1)} %convolution_subtract_fusion.13), custom_call_target="Cholesky" | custom-call | tf_op jit(solution)/shard_map/jit(cholesky)/cholesky | solution.py:71
  63.6 7.6 all-to-all-start
  75.3 53.6 %all-to-all-done = f32[16,256,256]{2,1,0:T(8,128)} async-done(((f32[16,256,256]{2,1,0:T(8,128)}), f32[16,256,256]{2,1,0:T(8,128)}, u32[]{:S(2)}, u32[]{:S(2)}) %all-to-all-start) | async-done | bytes 4194336 | tf_op jit(solution)/shard_map/all_to_all | solution.py:11
  131.7 11.7 %cholesky.568 = f32[128,128]{1,0:T(8,128)S(1)} custom-call(f32[128,128]{1,0:T(8,128)S(1)} %cholesky.811), custom_call_target="Cholesky" | custom-call | tf_op jit(solution)/shard_map/jit(cholesky)/cholesky | solution.py:76
  143.5 9.8 %custom-call.56 = f32[1,128,128]{1,2,0:T(8,128)S(1)} custom-call(f32[1,128,128]{2,1,0:T(8,128)S(1)} %get-tuple-element.387), custom_call_target="InvertDiagBlocksLowerTriangular" | custom-call | tf_op jit(solution)/shard_map/jit(cholesky)/cholesky | solution.py:76
  153.8 11.9 %cholesky.585 = f32[128,128]{1,0:T(8,128)S(1)} custom-call(f32[128,128]{1,0:T(8,128)S(1)} %convolution_subtract_fusion.12), custom_call_target="Cholesky" | custom-call | tf_op jit(solution)/shard_map/jit(cholesky)/cholesky | solution.py:76
  172.6 19.7 %custom-call.57 = f32[2,128,128]{1,2,0:T(8,128)S(1)} custom-call(f32[2,128,128]{2,1,0:T(8,128)S(1)} %get-tuple-element.207), custom_call_target="InvertDiagBlocksLowerTriangular" | custom-call | tf_op jit(solution)/shard_map/jit(_solve_triangular)/triangular_solve | solution.py:39
  193.4 22.2 %all_gather.21 = f32[256,512]{1,0:T(8,128)S(1)} all-gather(f32[16,512]{1,0:T(8,128)S(1)} %pad_maximum_fusion.4), channel_id=1, replica_groups=mesh['section'=16,'inner'=16] {'inner'}, dimensions={0}, use_global_device_ids=true | all-gather | bytes 557056 | tf_op jit(solution)/shard_map/all_gather | solution.py:25
  220.4 24.2 %all_gather.22 = f32[256,768]{1,0:T(8,128)S(1)} all-gather(f32[16,768]{1,0:T(8,128)S(1)} %pad_maximum_fusion.1), channel_id=1, replica_groups=mesh['section'=16,'inner'=16] {'inner'}, dimensions={0}, use_global_device_ids=true | all-gather | bytes 835584 | tf_op jit(solution)/shard_map/all_gather | solution.py:25
  248.4 12.5 %collective-permute-done.6 = f32[256,256]{0,1:T(8,128)S(1)} collective-permute-done((f32[256,256]{0,1:T(8,128)S(1)}, f32[256,256]{0,1:T(8,128)S(1)}, u32[]{:S(2)}, u32[]{:S(2)}) %collective-permute-start.6) | collective-permute-done | bytes 262176 | tf_op jit(solution)/shard_map/ppermute | solution.py:31
  261.2 11.7 %cholesky.602 = f32[128,128]{1,0:T(8,128)S(1)} custom-call(f32[128,128]{1,0:T(8,128)S(1)} %cholesky.814), custom_call_target="Cholesky" | custom-call | tf_op jit(solution)/shard_map/jit(cholesky)/cholesky | solution.py:71
  273.0 9.8 %custom-call.59 = f32[1,128,128]{1,2,0:T(8,128)S(1)} custom-call(f32[1,128,128]{2,1,0:T(8,128)S(1)} %get-tuple-element.383), custom_call_target="InvertDiagBlocksLowerTriangular" | custom-call | tf_op jit(solution)/shard_map/jit(cholesky)/cholesky | solution.py:71
  283.3 11.7 %cholesky.619 = f32[128,128]{1,0:T(8,128)S(1)} custom-call(f32[128,128]{1,0:T(8,128)S(1)} %slice_subtract_fusion.2), custom_call_target="Cholesky" | custom-call | tf_op jit(solution)/shard_map/jit(cholesky)/cholesky | solution.py:71
  301.4 7.1 all-to-all-start.1
  321.1 30.7 %all-to-all-done.1 = f32[16,256,256]{2,1,0:T(8,128)} async-done(((f32[16,256,256]{2,1,0:T(8,128)}), f32[16,256,256]{2,1,0:T(8,128)}, u32[]{:S(2)}, u32[]{:S(2)}) %all-to-all-start.1) | async-done | bytes 4194336 | tf_op jit(solution)/shard_map/all_to_all | solution.py:11
  354.6 11.7 %cholesky.636 = f32[128,128]{1,0:T(8,128)S(1)} custom-call(f32[128,128]{1,0:T(8,128)S(1)} %cholesky.817), custom_call_target="Cholesky" | custom-call | tf_op jit(solution)/shard_map/jit(cholesky)/cholesky | solution.py:76
  366.4 9.8 %custom-call.60 = f32[1,128,128]{1,2,0:T(8,128)S(1)} custom-call(f32[1,128,128]{2,1,0:T(8,128)S(1)} %get-tuple-element.379), custom_call_target="InvertDiagBlocksLowerTriangular" | custom-call | tf_op jit(solution)/shard_map/jit(cholesky)/cholesky | solution.py:76
  376.7 11.7 %cholesky.653 = f32[128,128]{1,0:T(8,128)S(1)} custom-call(f32[128,128]{1,0:T(8,128)S(1)} %convolution_subtract_fusion.11), custom_call_target="Cholesky" | custom-call | tf_op jit(solution)/shard_map/jit(cholesky)/cholesky | solution.py:76
  395.3 19.7 %custom-call.61 = f32[2,128,128]{1,2,0:T(8,128)S(1)} custom-call(f32[2,128,128]{2,1,0:T(8,128)S(1)} %get-tuple-element.209), custom_call_target="InvertDiagBlocksLowerTriangular" | custom-call | tf_op jit(solution)/shard_map/jit(_solve_triangular)/triangular_solve | solution.py:39
  416.1 22.9 %all_gather.23 = f32[256,512]{1,0:T(8,128)S(1)} all-gather(f32[16,512]{1,0:T(8,128)S(1)} %pad_maximum_fusion.5), channel_id=1, replica_groups=mesh['section'=16,'inner'=16] {'inner'}, dimensions={0}, use_global_device_ids=true | all-gather | bytes 557056 | tf_op jit(solution)/shard_map/all_gather | solution.py:25
  445.5 22.8 %all_gather.24 = f32[256,768]{1,0:T(8,128)S(1)} all-gather(f32[16,768]{1,0:T(8,128)S(1)} %pad_maximum_fusion.2), channel_id=1, replica_groups=mesh['section'=16,'inner'=16] {'inner'}, dimensions={0}, use_global_device_ids=true | all-gather | bytes 835584 | tf_op jit(solution)/shard_map/all_gather | solution.py:25
  473.6 9.0 collective-permute-done.9
  485.1 11.7 %cholesky.670 = f32[128,128]{1,0:T(8,128)S(1)} custom-call(f32[128,128]{1,0:T(8,128)S(1)} %cholesky.820), custom_call_target="Cholesky" | custom-call | tf_op jit(solution)/shard_map/jit(cholesky)/cholesky | solution.py:71
  497.4 10.4 %custom-call.63 = f32[1,128,128]{1,2,0:T(8,128)} custom-call(f32[1,128,128]{2,1,0:T(8,128)S(1)} %get-tuple-element.375), custom_call_target="InvertDiagBlocksLowerTriangular" | custom-call | tf_op jit(solution)/shard_map/jit(cholesky)/cholesky | solution.py:71
  510.0 11.7 %cholesky.687 = f32[128,128]{1,0:T(8,128)S(1)} custom-call(f32[128,128]{1,0:T(8,128)S(1)} %slice_subtract_fusion.1), custom_call_target="Cholesky" | custom-call | tf_op jit(solution)/shard_map/jit(cholesky)/cholesky | solution.py:71
  528.9 7.5 all-to-all-start.2
  551.1 21.3 %all-to-all-done.2 = f32[16,256,256]{2,1,0:T(8,128)} async-done(((f32[16,256,256]{2,1,0:T(8,128)}), f32[16,256,256]{2,1,0:T(8,128)}, u32[]{:S(2)}, u32[]{:S(2)}) %all-to-all-start.2) | async-done | bytes 4194336 | tf_op jit(solution)/shard_map/all_to_all | solution.py:11
  575.3 11.7 %cholesky.704 = f32[128,128]{1,0:T(8,128)S(1)} custom-call(f32[128,128]{1,0:T(8,128)S(1)} %cholesky.823), custom_call_target="Cholesky" | custom-call | tf_op jit(solution)/shard_map/jit(cholesky)/cholesky | solution.py:76
  587.1 9.8 %custom-call.64 = f32[1,128,128]{1,2,0:T(8,128)S(1)} custom-call(f32[1,128,128]{2,1,0:T(8,128)S(1)} %get-tuple-element.371), custom_call_target="InvertDiagBlocksLowerTriangular" | custom-call | tf_op jit(solution)/shard_map/jit(cholesky)/cholesky | solution.py:76
  597.4 11.7 %cholesky.721 = f32[128,128]{1,0:T(8,128)S(1)} custom-call(f32[128,128]{1,0:T(8,128)S(1)} %convolution_subtract_fusion.10), custom_call_target="Cholesky" | custom-call | tf_op jit(solution)/shard_map/jit(cholesky)/cholesky | solution.py:76
  611.9 5.6 while.52
  617.5 19.7 %custom-call.65 = f32[2,128,128]{1,2,0:T(8,128)S(1)} custom-call(f32[2,128,128]{2,1,0:T(8,128)S(1)} %get-tuple-element.211), custom_call_target="InvertDiagBlocksLowerTriangular" | custom-call | tf_op jit(solution)/shard_map/jit(_solve_triangular)/triangular_solve | solution.py:39
  638.3 21.9 %all_gather.25 = f32[256,512]{1,0:T(8,128)S(1)} all-gather(f32[16,512]{1,0:T(8,128)S(1)} %pad_maximum_fusion.6), channel_id=1, replica_groups=mesh['section'=16,'inner'=16] {'inner'}, dimensions={0}, use_global_device_ids=true | all-gather | bytes 557056 | tf_op jit(solution)/shard_map/all_gather | solution.py:25
  664.3 23.6 %all_gather.26 = f32[256,768]{1,0:T(8,128)S(1)} all-gather(f32[16,768]{1,0:T(8,128)S(1)} %pad_maximum_fusion.3), channel_id=1, replica_groups=mesh['section'=16,'inner'=16] {'inner'}, dimensions={0}, use_global_device_ids=true | all-gather | bytes 835584 | tf_op jit(solution)/shard_map/all_gather | solution.py:25
  690.7 106.4 %collective-permute-done.11 = f32[256,256]{0,1:T(8,128)S(1)} collective-permute-done((f32[256,256]{0,1:T(8,128)S(1)}, f32[256,256]{0,1:T(8,128)S(1)}, u32[]{:S(2)}, u32[]{:S(2)}) %collective-permute-start.11) | collective-permute-done | bytes 262176 | tf_op jit(solution)/shard_map/ppermute | solution.py:31
  798.0 11.7 %cholesky.738 = f32[128,128]{1,0:T(8,128)S(1)} custom-call(f32[128,128]{1,0:T(8,128)S(1)} %cholesky.826), custom_call_target="Cholesky" | custom-call | tf_op jit(solution)/shard_map/jit(cholesky)/cholesky | solution.py:71
  809.8 9.8 %custom-call.67 = f32[1,128,128]{1,2,0:T(8,128)S(1)} custom-call(f32[1,128,128]{2,1,0:T(8,128)S(1)} %get-tuple-element.367), custom_call_target="InvertDiagBlocksLowerTriangular" | custom-call | tf_op jit(solution)/shard_map/jit(cholesky)/cholesky | solution.py:71
  821.7 11.7 %cholesky.755 = f32[128,128]{1,0:T(8,128)S(1)} custom-call(f32[128,128]{1,0:T(8,128)S(1)} %slice_subtract_fusion), custom_call_target="Cholesky" | custom-call | tf_op jit(solution)/shard_map/jit(cholesky)/cholesky | solution.py:71
  839.7 7.1 all-to-all-start.3
  863.0 16.6 %all-to-all-done.3 = f32[16,256,256]{2,1,0:T(8,128)} async-done(((f32[16,256,256]{2,1,0:T(8,128)}), f32[16,256,256]{2,1,0:T(8,128)}, u32[]{:S(2)}, u32[]{:S(2)}) %all-to-all-start.3) | async-done | bytes 4194336 | tf_op jit(solution)/shard_map/all_to_all | solution.py:11
  882.4 11.7 %cholesky.772 = f32[128,128]{1,0:T(8,128)S(1)} custom-call(f32[128,128]{1,0:T(8,128)S(1)} %cholesky.829), custom_call_target="Cholesky" | custom-call | tf_op jit(solution)/shard_map/jit(cholesky)/cholesky | solution.py:76
  894.2 9.8 %custom-call.68 = f32[1,128,128]{1,2,0:T(8,128)S(1)} custom-call(f32[1,128,128]{2,1,0:T(8,128)S(1)} %get-tuple-element.363), custom_call_target="InvertDiagBlocksLowerTriangular" | custom-call | tf_op jit(solution)/shard_map/jit(cholesky)/cholesky | solution.py:76
  904.5 11.7 %cholesky.789 = f32[128,128]{1,0:T(8,128)S(1)} custom-call(f32[128,128]{1,0:T(8,128)S(1)} %convolution_subtract_fusion.9), custom_call_target="Cholesky" | custom-call | tf_op jit(solution)/shard_map/jit(cholesky)/cholesky | solution.py:76
  923.4 19.7 %custom-call.69 = f32[2,128,128]{1,2,0:T(8,128)S(1)} custom-call(f32[2,128,128]{2,1,0:T(8,128)S(1)} %get-tuple-element.213), custom_call_target="InvertDiagBlocksLowerTriangular" | custom-call | tf_op jit(solution)/shard_map/jit(_solve_triangular)/triangular_solve | solution.py:39
  946.6 22.4 %all_gather.27 = f32[256,512]{1,0:T(8,128)S(1)} all-gather(f32[16,512]{1,0:T(8,128)S(1)} %pad_maximum_fusion.7), channel_id=1, replica_groups=mesh['section'=16,'inner'=16] {'inner'}, dimensions={0}, use_global_device_ids=true | all-gather | bytes 557056 | tf_op jit(solution)/shard_map/all_gather | solution.py:25
  (431 shorter events, 176.3 us)
Async XLA Ops:
  0.6 15.6 %copy-start = (f32[256,256]{1,0:T(8,128)S(1)}, f32[256,256]{1,0:T(8,128)}, u32[]{:S(2)}) copy-start(f32[256,256]{1,0:T(8,128)} %param.18) | copy-start | bytes 786436
  0.6 15.6 %copy-start.1 = (f32[256,256]{1,0:T(8,128)S(1)}, f32[256,256]{1,0:T(8,128)}, u32[]{:S(2)}) copy-start(f32[256,256]{1,0:T(8,128)} %param.25) | copy-start | bytes 786436
  0.6 15.6 %copy-start.18 = (f32[256]{0:T(256)S(1)}, f32[256]{0:T(256)}, u32[]{:S(2)}) copy-start(f32[256]{0:T(256)} %param.26) | copy-start | bytes 3076
  0.7 11.5 %collective-permute-start = (f32[1,256]{1,0:T(1,128)}, f32[1,256]{1,0:T(1,128)S(1)}, u32[]{:S(2)}, u32[]{:S(2)}) collective-permute-start(f32[1,256]{1,0:T(1,128)} %param.21), channel_id=1, source_target_pairs={{16,0},{32,16},{48,32},{64,48},{80,64},{96,80},{112,96},{128,112},... | collective-permute-start | bytes 3080 | tf_op jit(solution)/shard_map/ppermute | solution.py:31
  2.1 12.2 %collective-permute-start.3 = (f32[1,256]{1,0:T(1,128)}, f32[1,256]{1,0:T(1,128)S(1)}, u32[]{:S(2)}, u32[]{:S(2)}) collective-permute-start(f32[1,256]{1,0:T(1,128)} %param.23), channel_id=1, source_target_pairs={{16,0},{32,16},{48,32},{64,48},{80,64},{96,80},{112,96},{128,112},... | collective-permute-start | bytes 3080 | tf_op jit(solution)/shard_map/ppermute | solution.py:31
  3.4 12.2 %collective-permute-start.2 = (f32[1,256]{1,0:T(1,128)}, f32[1,256]{1,0:T(1,128)S(1)}, u32[]{:S(2)}, u32[]{:S(2)}) collective-permute-start(f32[1,256]{1,0:T(1,128)} %param.24), channel_id=1, source_target_pairs={{16,0},{32,16},{48,32},{64,48},{80,64},{96,80},{112,96},{128,112},... | collective-permute-start | bytes 3080 | tf_op jit(solution)/shard_map/ppermute | solution.py:31
  4.7 10.8 %collective-permute-start.1 = (f32[1,256]{1,0:T(1,128)}, f32[1,256]{1,0:T(1,128)S(1)}, u32[]{:S(2)}, u32[]{:S(2)}) collective-permute-start(f32[1,256]{1,0:T(1,128)} %param.20), channel_id=1, source_target_pairs={{16,0},{32,16},{48,32},{64,48},{80,64},{96,80},{112,96},{128,112},... | collective-permute-start | bytes 3080 | tf_op jit(solution)/shard_map/ppermute | solution.py:31
  6.0 10.2 %collective-permute-start.4 = (f32[1,256]{1,0:T(1,128)}, f32[1,256]{1,0:T(1,128)S(1)}, u32[]{:S(2)}, u32[]{:S(2)}) collective-permute-start(f32[1,256]{1,0:T(1,128)} %param.22), channel_id=1, source_target_pairs={{16,0},{32,16},{48,32},{64,48},{80,64},{96,80},{112,96},{128,112},... | collective-permute-start | bytes 3080 | tf_op jit(solution)/shard_map/ppermute | solution.py:31
  24.6 48.0 %copy-start.16 = (f32[256]{0:T(256)}, f32[256]{0:T(256)S(1)}, u32[]{:S(2)}) copy-start(f32[256]{0:T(256)S(1)} %get-tuple-element.30) | copy-start | bytes 3076
  63.6 65.2 %all-to-all-start = ((f32[16,256,256]{2,1,0:T(8,128)}), f32[16,256,256]{2,1,0:T(8,128)}, u32[]{:S(2)}, u32[]{:S(2)}) async-start(f32[16,256,256]{2,1,0:T(8,128)} %broadcast_in_dim.60), calls=%async_computation | async-start | bytes 8388608 | tf_op jit(solution)/shard_map/all_to_all | solution.py:11
  172.0 0.6 copy-start.19
  216.8 223.3 %collective-permute-start.7 = (f32[16,256]{0,1:T(8,128)S(1)}, f32[16,256]{0,1:T(8,128)}, u32[]{:S(2)}, u32[]{:S(2)}) collective-permute-start(f32[16,256]{0,1:T(8,128)S(1)} %fusion.63), channel_id=1, source_target_pairs={{32,0},{48,16},{64,32},{80,48},{96,64},{112,80},{128,96},{144,112}... | collective-permute-start | bytes 49160 | tf_op jit(solution)/shard_map/ppermute | solution.py:31
  245.6 15.4 %collective-permute-start.6 = (f32[256,256]{0,1:T(8,128)S(1)}, f32[256,256]{0,1:T(8,128)S(1)}, u32[]{:S(2)}, u32[]{:S(2)}) collective-permute-start(f32[256,256]{0,1:T(8,128)S(1)} %copy.170), channel_id=1, source_target_pairs={{32,0},{48,16},{64,32},{80,48},{96,64},{112,80},{128,96},{144,112}... | collective-permute-start | bytes 786440 | tf_op jit(solution)/shard_map/ppermute | solution.py:31
  301.4 7.1 copy-start.8
  301.4 7.3 copy-start.10
  301.4 8.6 copy-start.17
  301.4 10.2 %copy-start.6 = (f32[256,256]{1,0:T(8,128)S(1)}, f32[256,256]{1,0:T(8,128)}, u32[]{:S(2)}) copy-start(f32[256,256]{1,0:T(8,128)} %get-tuple-element.357) | copy-start | bytes 786436
  301.4 50.4 %all-to-all-start.1 = ((f32[16,256,256]{2,1,0:T(8,128)}), f32[16,256,256]{2,1,0:T(8,128)}, u32[]{:S(2)}, u32[]{:S(2)}) async-start(f32[16,256,256]{2,1,0:T(8,128)} %broadcast_in_dim.61), calls=%async_computation.1 | async-start | bytes 8388608 | tf_op jit(solution)/shard_map/all_to_all | solution.py:11
  310.1 44.5 %copy-start.14 = (f32[256]{0:T(256)}, f32[256]{0:T(256)S(1)}, u32[]{:S(2)}) copy-start(f32[256]{0:T(256)S(1)} %add_select_fusion.6) | copy-start | bytes 3076
  310.1 5.6 collective-permute-start.13
  311.6 9.0 collective-permute-start.5
  316.7 228.1 %collective-permute-start.15 = (f32[256]{0:T(256)S(1)}, f32[256]{0:T(256)}, u32[]{:S(2)}, u32[]{:S(2)}) collective-permute-start(f32[256]{0:T(256)S(1)} %get-tuple-element.324), channel_id=1, source_target_pairs={{32,0},{48,16},{64,32},{80,48},{96,64},{112,80},{128,96},{144,112}... | collective-permute-start | bytes 3080 | tf_op jit(solution)/shard_map/ppermute | solution.py:31
  321.1 70.0 %copy-start.20 = (s32[2,2]{1,0:T(2,128)S(1)}, s32[2,2]{1,0:T(2,128)}, u32[]{:S(2)}) copy-start(s32[2,2]{1,0:T(2,128)} %copy-done.19) | copy-start | bytes 52
  441.4 221.5 %collective-permute-start.10 = (f32[16,256]{0,1:T(8,128)S(1)}, f32[16,256]{0,1:T(8,128)}, u32[]{:S(2)}, u32[]{:S(2)}) collective-permute-start(f32[16,256]{0,1:T(8,128)S(1)} %fusion.59), channel_id=1, source_target_pairs={{64,0},{80,16},{96,32},{112,48},{128,64},{144,80},{160,96},{176,11... | collective-permute-start | bytes 49160 | tf_op jit(solution)/shard_map/ppermute | solution.py:31
  445.4 79.7 %copy-start.2 = (f32[16,256]{0,1:T(8,128)}, f32[16,256]{0,1:T(8,128)S(1)}, u32[]{:S(2)}) copy-start(f32[16,256]{0,1:T(8,128)S(1)} %fusion.60) | copy-start | bytes 49156
  470.0 12.5 %collective-permute-start.9 = (f32[256,256]{0,1:T(8,128)}, f32[256,256]{0,1:T(8,128)S(1)}, u32[]{:S(2)}, u32[]{:S(2)}) collective-permute-start(f32[256,256]{0,1:T(8,128)} %copy.171), channel_id=1, source_target_pairs={{64,0},{80,16},{96,32},{112,48},{128,64},{144,80},{160,96},{176,11... | collective-permute-start | bytes 786440 | tf_op jit(solution)/shard_map/ppermute | solution.py:31
  484.4 0.7 copy-start.4
  528.9 7.6 copy-start.9
  528.9 7.7 copy-start.11
  528.9 9.1 copy-start.15
  528.9 43.5 %all-to-all-start.2 = ((f32[16,256,256]{2,1,0:T(8,128)}), f32[16,256,256]{2,1,0:T(8,128)}, u32[]{:S(2)}, u32[]{:S(2)}) async-start(f32[16,256,256]{2,1,0:T(8,128)} %broadcast_in_dim.62), calls=%async_computation.2 | async-start | bytes 8388608 | tf_op jit(solution)/shard_map/all_to_all | solution.py:11
  538.1 6.7 copy-start.12
  538.1 6.4 collective-permute-start.14
  539.4 11.2 %collective-permute-start.8 = (f32[256,256]{1,0:T(8,128)}, f32[256,256]{1,0:T(8,128)S(1)}, u32[]{:S(2)}, u32[]{:S(2)}) collective-permute-start(f32[256,256]{1,0:T(8,128)} %get-tuple-element.354), channel_id=1, source_target_pairs={{64,0},{80,16},{96,32},{112,48},{128,64},{144,80},{160,96},{176,11... | collective-permute-start | bytes 786440 | tf_op jit(solution)/shard_map/ppermute | solution.py:31
  545.9 306.1 %collective-permute-start.17 = (f32[256]{0:T(256)}, f32[256]{0:T(256)}, u32[]{:S(2)}, u32[]{:S(2)}) collective-permute-start(f32[256]{0:T(256)} %get-tuple-element.322), channel_id=1, source_target_pairs={{64,0},{80,16},{96,32},{112,48},{128,64},{144,80},{160,96},{176,11... | collective-permute-start | bytes 3080 | tf_op jit(solution)/shard_map/ppermute | solution.py:31
  574.9 87.1 %copy-start.3 = (f32[16,256]{0,1:T(8,128)S(1)}, f32[16,256]{0,1:T(8,128)}, u32[]{:S(2)}) copy-start(f32[16,256]{0,1:T(8,128)} %copy-done.2) | copy-start | bytes 49156
  688.9 108.2 %collective-permute-start.11 = (f32[256,256]{0,1:T(8,128)S(1)}, f32[256,256]{0,1:T(8,128)S(1)}, u32[]{:S(2)}, u32[]{:S(2)}) collective-permute-start(f32[256,256]{0,1:T(8,128)S(1)} %copy.172), channel_id=1, source_target_pairs={{128,0},{144,16},{160,32},{176,48},{192,64},{208,80},{224,96},{240... | collective-permute-start | bytes 786440 | tf_op jit(solution)/shard_map/ppermute | solution.py:31
  797.3 0.7 copy-start.5
  839.7 9.1 copy-start.13
  839.7 10.5 %copy-start.7 = (f32[256,256]{1,0:T(8,128)S(1)}, f32[256,256]{1,0:T(8,128)}, u32[]{:S(2)}) copy-start(f32[256,256]{1,0:T(8,128)} %get-tuple-element.351) | copy-start | bytes 786436
  839.7 39.8 %all-to-all-start.3 = ((f32[16,256,256]{2,1,0:T(8,128)}), f32[16,256,256]{2,1,0:T(8,128)}, u32[]{:S(2)}, u32[]{:S(2)}) async-start(f32[16,256,256]{2,1,0:T(8,128)} %broadcast_in_dim.63), calls=%async_computation.3 | async-start | bytes 8388608 | tf_op jit(solution)/shard_map/all_to_all | solution.py:11
  848.9 9.4 collective-permute-start.16
  850.2 12.3 %collective-permute-start.12 = (f32[256,256]{1,0:T(8,128)S(1)}, f32[256,256]{1,0:T(8,128)S(1)}, u32[]{:S(2)}, u32[]{:S(2)}) collective-permute-start(f32[256,256]{1,0:T(8,128)S(1)} %copy-done.7), channel_id=1, source_target_pairs={{128,0},{144,16},{160,32},{176,48},{192,64},{208,80},{224,96},{240... | collective-permute-start | bytes 786440 | tf_op jit(solution)/shard_map/ppermute | solution.py:31
  863.0 56.0 %copy-start.21 = (s32[2,2]{1,0:T(2,128)S(1)}, s32[2,2]{1,0:T(2,128)}, u32[]{:S(2)}) copy-start(s32[2,2]{1,0:T(2,128)} %get-tuple-element.680) | copy-start | bytes 52
where the time goes:
time: 984 us; the launch traced here: 970 us
  other arithmetic  375 us (38%)
  waiting for transfers between devices  266 us (27%)
  blocking collectives  160 us (16%)
  matrix products  56.9 us (6%)
  starting transfers between devices  53.7 us (5%)
  local copies, waits for them, and re-layouts  37.2 us (4%)
  between operations  12.7 us (1%)
    all_gather x7, blocking collectives, in_one_piece(): lax.all_gather(both, axis, axis=dim, tiled=True)  160 us
    ppermute x18, waiting for transfers between devices, from_behind(): lax.ppermute(value, axis, [(source, source + steps) for source in range(l...  144 us
    another operation x27, other arithmetic, combine(): factor_j = jnp.linalg.cholesky(hess_up)  140 us
    another operation x28, other arithmetic, combine(): factor_m = jnp.linalg.cholesky(identity + gram)  139 us
    all_to_all x4, waiting for transfers between devices, from_everyone(): return lax.all_to_all(copies, axis, split_axis=0, concat_axis=0, tiled=True)  122 us
    another operation x16, other arithmetic, lower_solve(): return jax.scipy.linalg.solve_triangular(factor, target, lower=True)  78.8 us
    dot_general x75, matrix products, matmul(): return jnp.dot(first_mat, second_mat, precision=highest)  36.4 us
    all_to_all x4, starting transfers between devices, from_everyone(): return lax.all_to_all(copies, axis, split_axis=0, concat_axis=0, tiled=True)  29.3 us
  transfers between devices with their start and end apart: 22, of which 12 were waited for; matrix products, arithmetic and copies ran while one was open for 31% of the time, Pallas kernels for 0%

commit v1 on v0

v1 whole, which is shorter than its diff:
```python
import jax
import jax.numpy as jnp
from jax import lax
from jax.experimental import pallas as pl
from jax.experimental.pallas import tpu as pltpu
from jax.sharding import PartitionSpec as P

f32, bf16 = jnp.float32, jnp.bfloat16
N = 256
PHASES = 16
highest = lax.Precision.HIGHEST


def split(x):
    head = x.astype(bf16)
    return head, (x - head.astype(f32)).astype(bf16)


def dot(a, b):
    return jnp.dot(a, b, preferred_element_type=f32)


def dot3(a, b):
    (ah, al), (bh, bl) = a, b
    return dot(ah, bh) + (dot(ah, bl) + dot(al, bh))


def exact(a, b):
    return jnp.dot(a, b, precision=highest, preferred_element_type=f32)


def square_sum(x):
    return jnp.sum(jnp.sum(x * x, axis=0, keepdims=True), axis=1, keepdims=True)


def kernel(
    g_ref, plant_ref, act_ref, term_ref, tgrad_ref, hess_ref, grad_ref,
    ph_ref, plo_ref, pt_ref, pth_ref, ath_ref, atl_ref, apa_ref, eye_ref, drift_ref,
    kh_ref, kl_ref, th_ref, tl_ref, bh_ref, bl_ref, s_ref, lin_ref, bad_ref, e_ref, x_ref,
):
    section = lax.axis_index("section")
    inner = lax.axis_index("inner")
    plant = plant_ref[...]
    act = act_ref[...]
    ph_ref[...], plo_ref[...] = split(plant)
    plant_t = plant.T
    pt_ref[...] = plant_t
    pth_ref[...] = plant_t.astype(bf16)
    act_t = act.T
    ath_ref[...], atl_ref[...] = split(act_t)
    apa_ref[pl.ds(0, N), :] = act
    apa_ref[pl.ds(N, N), :] = exact(plant, act)
    rows = lax.broadcasted_iota(jnp.int32, (N, N), 0)
    cols = lax.broadcasted_iota(jnp.int32, (N, N), 1)
    eye_ref[...] = jnp.where(rows == cols, 1.0, 0.0).astype(f32)
    drift_ref[...] = g_ref[:, 4, :] - exact(g_ref[:, 3, :] / g_ref[:, 1, :], act_t)

    def start():
        eye = eye_ref[...]
        scaled = apa_ref[pl.ds(0, N), :] / g_ref[PHASES - 1][1:2]
        s = dot3(split(scaled), (ath_ref[...], atl_ref[...]))
        kh_ref[...], kl_ref[...] = split(dot3(split(term_ref[...]), split(s)))
        lin_ref[...] = -jnp.sum(eye * tgrad_ref[...], axis=1, keepdims=True)
        bad_ref[...] = jnp.zeros((1, 1), f32)

    def quick(levels):
        eye, pt = eye_ref[...], pt_ref[...]
        kh, kl = kh_ref[...], kl_ref[...]
        k = kh.astype(f32) + kl.astype(f32)
        first = dot(jnp.concatenate([kh, pth_ref[...]], axis=0), kh)
        mu = jnp.sqrt(square_sum(k)) * 0.25
        al = 2.0 / (2.0 + mu)
        rho = mu * al * 0.5
        c = 2.0 / (2.0 - rho * rho)
        x = eye * (c * al * (2.0 - al)) - (c * al * al) * k
        t = (c * al * (2.0 - al)) * pt - (c * al * al) * first[N:]
        e = eye * (1.0 - c + c * (1.0 - al) * (1.0 - al)) - (2.0 * c * al * (1.0 - al)) * k
        e = e + (c * al * al) * first[:N]
        for _ in range(1, levels):
            rho = rho * rho / (2.0 - rho * rho)
            c = 2.0 / (2.0 - rho * rho)
            eh = e.astype(bf16)
            product = dot(jnp.concatenate([eh, x.astype(bf16), t.astype(bf16)], axis=0), eh)
            e = (1.0 - c) * eye + c * product[:N]
            x = c * (x + product[N : 2 * N])
            t = c * (t + product[2 * N :])
        guess = t.astype(bf16)
        t = guess.astype(f32)
        residue = pt - t - (dot(guess, kh) + dot(guess, kl))
        good = (square_sum(e) < 2.5e-3) & (square_sum(residue) < 4e-4 * square_sum(t))
        bad_ref[...] += jnp.where(good, 0.0, 1.0)
        return t + dot(residue.astype(bf16), x.astype(bf16))

    def careful():
        eye, pt = eye_ref[...], pt_ref[...]
        k = kh_ref[...].astype(f32) + kl_ref[...].astype(f32)
        mu = jnp.minimum(jnp.sqrt(jnp.sum(k * k)), jnp.max(jnp.sum(jnp.abs(k), axis=1)))
        al = 2.0 / (2.0 + mu)
        x_ref[...] = al * eye
        e_ref[...] = (1.0 - al) * eye - al * k

        def going(state):
            step, _, size = state
            return (step < 64) & (size > 1e-6)

        def level(state):
            step, rho, _ = state
            c = 2.0 / (2.0 - rho * rho)
            e = e_ref[...]
            x_ref[...] = c * (x_ref[...] + exact(x_ref[...], e))
            e = (1.0 - c) * eye_ref[...] + c * exact(e, e)
            e_ref[...] = e
            return step + 1, rho * rho / (2.0 - rho * rho), jnp.sum(e * e)

        lax.while_loop(going, level, (jnp.int32(0), mu * al * 0.5, jnp.float32(1.0)))
        e_ref[...] = exact(pt, x_ref[...])

        def refine(_, carry):
            k = kh_ref[...].astype(f32) + kl_ref[...].astype(f32)
            t = e_ref[...]
            e_ref[...] = t + exact(pt_ref[...] - t - exact(t, k), x_ref[...])
            return carry

        lax.fori_loop(0, 3, refine, 0)
        return e_ref[...]

    def phase(k, solve, hess):
        now = g_ref[k]
        ahead = g_ref[jnp.maximum(k - 1, 0)]
        eye = eye_ref[...]
        hs = split(hess)
        b = split(dot3(hs, (ph_ref[...], plo_ref[...])))
        spreads = dot3(split(apa_ref[...] / ahead[1:2]), (ath_ref[...], atl_ref[...]))
        c = dot3(hs, split(spreads[N:]))
        t = solve()
        ts = split(t)
        weights = jnp.sum(eye * now[0:1], axis=1, keepdims=True)
        kh_ref[...], kl_ref[...] = split(dot3(ts, split(c)) + weights * spreads[:N])
        th_ref[...], tl_ref[...] = ts
        bh_ref[...], bl_ref[...] = b
        column = lin_ref[...] - jnp.sum(hess * drift_ref[pl.ds(k, 1), :], axis=1, keepdims=True)
        row = jnp.sum(eye * column, axis=0, keepdims=True)
        lin_ref[...] = jnp.sum(t * row - eye * now[2:3], axis=1, keepdims=True)

    def stored_hess(k):
        product = dot3((th_ref[...], tl_ref[...]), (bh_ref[...], bl_ref[...]))
        return product + eye_ref[...] * g_ref[k][0:1]

    def sweep(solve_first, solve):
        start()
        phase(PHASES - 1, solve_first, term_ref[...])

        def body(i, carry):
            k = PHASES - 1 - i
            phase(k, solve, stored_hess(k + 1))
            return carry

        lax.fori_loop(1, PHASES - section, body, 0)

    sweep(lambda: quick(4), lambda: quick(3))

    @pl.when(jnp.max(bad_ref[...]) > 0.0)
    def _():
        sweep(careful, careful)

    height = hess_ref.shape[0]
    at = pl.multiple_of(inner * height, height)
    mine = pl.ds(at, height)
    product = dot3((th_ref[mine, :], tl_ref[mine, :]), (bh_ref[...], bl_ref[...]))
    hess_ref[...] = product + eye_ref[mine, :] * g_ref[section][0:1]
    row = jnp.sum(eye_ref[...] * lin_ref[...], axis=0, keepdims=True)
    turned = pltpu.roll(jnp.broadcast_to(-row, (8, N)), lax.rem(N - at, N), 1)
    grad_ref[...] = turned[0:1, :height]


def on_device(plant, actuation, state_weight, input_weight, state_grad, input_grad, defect, terminal_hess, terminal_grad):
    height = N // lax.axis_size("inner")
    zero = jnp.zeros((3, N), f32)
    own = jnp.concatenate([state_weight, input_weight, state_grad, input_grad, defect, zero], axis=0)
    copies = jnp.broadcast_to(own[None], (PHASES, 8, N))
    gathered = lax.all_to_all(copies, "section", split_axis=0, concat_axis=0, tiled=True)
    full = lambda dtype: pltpu.VMEM((N, N), dtype)
    hess, grad = pl.pallas_call(
        kernel,
        out_shape=(jax.ShapeDtypeStruct((height, N), f32), jax.ShapeDtypeStruct((1, height), f32)),
        in_specs=[pl.BlockSpec(memory_space=pltpu.VMEM)] * 5,
        out_specs=(pl.BlockSpec(memory_space=pltpu.VMEM),) * 2,
        scratch_shapes=[
            full(bf16), full(bf16), full(f32), full(bf16), full(bf16), full(bf16),
            pltpu.VMEM((2 * N, N), f32), full(f32), pltpu.VMEM((PHASES, N), f32),
            full(bf16), full(bf16), full(bf16), full(bf16), full(bf16), full(bf16),
            full(f32), pltpu.VMEM((N, 1), f32), pltpu.VMEM((1, 1), f32), full(f32), full(f32),
        ],
    )(gathered, plant, actuation, terminal_hess, terminal_grad[None])
    return hess[None], grad


def solution(mesh):
    data = P("section", None)
    in_specs = (P(), P(), data, data, data, data, data, P(), P())
    out_specs = (P("section", "inner", None), P("section", "inner"))
    return jax.shard_map(on_device, mesh=mesh, in_specs=in_specs, out_specs=out_specs, check_vma=False)
```

time: 984 us -> 194 us (0.20); the launches traced: 970 us -> 193 us
  other arithmetic: 375 us -> 0 us
  waiting for transfers between devices: 266 us -> 0 us
  Pallas kernels: 0 us -> 174 us
  blocking collectives: 160 us -> 17.1 us
  matrix products: 56.9 us -> 0 us
  starting transfers between devices: 53.7 us -> 0 us
  local copies, waits for them, and re-layouts: 37.2 us -> 1.4 us
  between operations: 12.7 us -> 0.67 us
    another operation x71 -> x0, other arithmetic: 357 us -> none  [the longest x27 140 us: combine(): factor_j = jnp.linalg.cholesky(hess_up)]
    pallas_call x0 -> x1, Pallas kernels: none -> 174 us  [on_device(): pl.pallas_call(kernel, out_shape=(jax.ShapeDtypeStruct((height, N), f32),...]
    all_gather x7 -> x0, blocking collectives: 160 us -> none  [in_one_piece(): lax.all_gather(both, axis, axis=dim, tiled=True)]
    ppermute x18 -> x0, waiting for transfers between devices: 144 us -> none  [from_behind(): lax.ppermute(value, axis, [(source, source + steps) for source in range(l...]
    all_to_all x4 -> x0, waiting for transfers between devices: 122 us -> none  [from_everyone(): return lax.all_to_all(copies, axis, split_axis=0, concat_axis=0, tiled=True)]
    dot_general x75 -> x0, matrix products: 36.4 us -> none  [matmul(): return jnp.dot(first_mat, second_mat, precision=highest)]
    all_to_all x4 -> x0, starting transfers between devices: 29.3 us -> none  [from_everyone(): return lax.all_to_all(copies, axis, split_axis=0, concat_axis=0, tiled=True)]
    ppermute x18 -> x0, starting transfers between devices: 24.4 us -> none  [from_behind(): lax.ppermute(value, axis, [(source, source + steps) for source in range(l...]
  transfers between devices with their start and end apart: 22 -> 0, of which waited for: 12 -> 0; matrix products, arithmetic and copies ran while one was open for 31% -> 0% of each run, Pallas kernels for 0% -> 0%
where the time goes in v1:
time: 194 us; the launch traced here: 193 us
  Pallas kernels  174 us (90%)
  blocking collectives  17.1 us (9%)
    pallas_call x1, Pallas kernels, on_device(): pl.pallas_call(kernel, out_shape=(jax.ShapeDtypeStruct((height, N), f32),...  174 us
    all_to_all x1, blocking collectives, on_device(): lax.all_to_all(copies, 'section', split_axis=0, concat_axis=0, tiled=True)  17.1 us

profile of v1, /device:TPU:22, one launch (start us, length us, event | category | flops | bytes accessed | tf_op | source)
XLA Modules:
  0.0 193.3 jit_solution(8385228821180164881)
XLA Ops:
  0.6 0.0 copy-start.3
  0.6 0.0 copy-start.2
  0.7 0.0 copy-start.1
  0.7 0.0 copy-start
  0.7 0.6 copy-done.3
  1.3 0.0 copy-done.2
  1.3 0.0 copy-done.1
  1.3 0.0 copy-done
  1.4 0.7 concatenate.3
  2.1 17.1 %all_to_all.5.g_ref = f32[16,8,256]{2,1,0:T(8,128)} all-to-all(f32[16,8,256]{2,1,0:T(8,128)S(1)} %broadcast_in_dim.16), channel_id=1, replica_groups=mesh['section'=16,'inner'=16] {'section'}, dimensions={0} | all-to-all | bytes 262144 | tf_op jit(solution)/shard_map/all_to_all | solution.py:181
  19.2 174.1 %shard_map.104 = (f32[16,256]{1,0:T(8,128)}, f32[1,16]{1,0:T(1,128)}) custom-call(f32[16,8,256]{2,1,0:T(8,128)} %all_to_all.5.g_ref, f32[256,256]{1,0:T(8,128)} %plant_ref.1, f32[256,256]{1,0:T(8,128)} %act_ref.1, f32[256,256]{1,0:T(8,128)} %term_ref.1, f32[1,256]{1,0:T(1,128)} %bitcast.2), custom_call_target="tpu_custom_call" | custom-call | tf_op jit(solution)/shard_map/pallas_call | solution.py:183
  (2 shorter events, 0.0 us)
Async XLA Ops:
  0.6 0.7 copy-start.3
  0.6 0.7 copy-start.2
  0.7 0.7 copy-start.1
  0.7 0.7 copy-start

commit v2 on v1

--- a/solution.py
+++ b/solution.py
@@ -63,11 +63,12 @@
         lin_ref[...] = -jnp.sum(eye * tgrad_ref[...], axis=1, keepdims=True)
         bad_ref[...] = jnp.zeros((1, 1), f32)
 
-    def quick(levels):
+    def quick(levels, beside):
         eye, pt = eye_ref[...], pt_ref[...]
         kh, kl = kh_ref[...], kl_ref[...]
+        first = dot(jnp.concatenate([kh, pth_ref[...]], axis=0), kh)
+        next(beside)
         k = kh.astype(f32) + kl.astype(f32)
-        first = dot(jnp.concatenate([kh, pth_ref[...]], axis=0), kh)
         mu = jnp.sqrt(square_sum(k)) * 0.25
         al = 2.0 / (2.0 + mu)
         rho = mu * al * 0.5
@@ -76,43 +77,45 @@
         t = (c * al * (2.0 - al)) * pt - (c * al * al) * first[N:]
         e = eye * (1.0 - c + c * (1.0 - al) * (1.0 - al)) - (2.0 * c * al * (1.0 - al)) * k
         e = e + (c * al * al) * first[:N]
-        for _ in range(1, levels):
+        for level in range(1, levels):
             rho = rho * rho / (2.0 - rho * rho)
             c = 2.0 / (2.0 - rho * rho)
             eh = e.astype(bf16)
             product = dot(jnp.concatenate([eh, x.astype(bf16), t.astype(bf16)], axis=0), eh)
+            if level < 3:
+                next(beside)
             e = (1.0 - c) * eye + c * product[:N]
             x = c * (x + product[N : 2 * N])
             t = c * (t + product[2 * N :])
         guess = t.astype(bf16)
         t = guess.astype(f32)
         residue = pt - t - (dot(guess, kh) + dot(guess, kl))
+        next(beside)
         good = (square_sum(e) < 2.5e-3) & (square_sum(residue) < 4e-4 * square_sum(t))
         bad_ref[...] += jnp.where(good, 0.0, 1.0)
-        return t + dot(residue.astype(bf16), x.astype(bf16))
-
-    def careful():
+        t = t + dot(residue.astype(bf16), x.astype(bf16))
+        next(beside)
+        return t
+
+    def careful(beside):
+        for _ in range(5):
+            next(beside)
         eye, pt = eye_ref[...], pt_ref[...]
         k = kh_ref[...].astype(f32) + kl_ref[...].astype(f32)
-        mu = jnp.minimum(jnp.sqrt(jnp.sum(k * k)), jnp.max(jnp.sum(jnp.abs(k), axis=1)))
+        most = jnp.max(jnp.sum(jnp.abs(k), axis=1, keepdims=True), axis=0, keepdims=True)
+        mu = jnp.minimum(jnp.sqrt(square_sum(k)), most)
         al = 2.0 / (2.0 + mu)
         x_ref[...] = al * eye
         e_ref[...] = (1.0 - al) * eye - al * k
 
-        def going(state):
-            step, _, size = state
-            return (step < 64) & (size > 1e-6)
-
-        def level(state):
-            step, rho, _ = state
+        def level(_, rho):
             c = 2.0 / (2.0 - rho * rho)
             e = e_ref[...]
             x_ref[...] = c * (x_ref[...] + exact(x_ref[...], e))
-            e = (1.0 - c) * eye_ref[...] + c * exact(e, e)
-            e_ref[...] = e
-            return step + 1, rho * rho / (2.0 - rho * rho), jnp.sum(e * e)
-
-        lax.while_loop(going, level, (jnp.int32(0), mu * al * 0.5, jnp.float32(1.0)))
+            e_ref[...] = (1.0 - c) * eye_ref[...] + c * exact(e, e)
+            return rho * rho / (2.0 - rho * rho)
+
+        lax.fori_loop(0, 24, level, mu * al * 0.5)
         e_ref[...] = exact(pt, x_ref[...])
 
         def refine(_, carry):
@@ -124,23 +127,35 @@
         lax.fori_loop(0, 3, refine, 0)
         return e_ref[...]
 
-    def phase(k, solve, hess):
+    def phase(k, solve, first):
         now = g_ref[k]
         ahead = g_ref[jnp.maximum(k - 1, 0)]
         eye = eye_ref[...]
-        hs = split(hess)
-        b = split(dot3(hs, (ph_ref[...], plo_ref[...])))
-        spreads = dot3(split(apa_ref[...] / ahead[1:2]), (ath_ref[...], atl_ref[...]))
-        c = dot3(hs, split(spreads[N:]))
-        t = solve()
+        found = {}
+
+        def beside():
+            hess = term_ref[...] if first else stored_hess(k + 1)
+            yield
+            act_t = ath_ref[...], atl_ref[...]
+            found["ps"] = split(dot3(split(apa_ref[pl.ds(N, N), :] / ahead[1:2]), act_t))
+            yield
+            found["s"] = dot3(split(apa_ref[pl.ds(0, N), :] / ahead[1:2]), act_t)
+            hs = split(hess)
+            yield
+            found["c"] = split(dot3(hs, found["ps"]))
+            yield
+            found["b"] = split(dot3(hs, (ph_ref[...], plo_ref[...])))
+            column = lin_ref[...] - jnp.sum(hess * drift_ref[pl.ds(k, 1), :], axis=1, keepdims=True)
+            found["row"] = jnp.sum(eye * column, axis=0, keepdims=True)
+            yield
+
+        t = solve(beside())
         ts = split(t)
         weights = jnp.sum(eye * now[0:1], axis=1, keepdims=True)
-        kh_ref[...], kl_ref[...] = split(dot3(ts, split(c)) + weights * spreads[:N])
+        kh_ref[...], kl_ref[...] = split(dot3(ts, found["c"]) + weights * found["s"])
         th_ref[...], tl_ref[...] = ts
-        bh_ref[...], bl_ref[...] = b
-        column = lin_ref[...] - jnp.sum(hess * drift_ref[pl.ds(k, 1), :], axis=1, keepdims=True)
-        row = jnp.sum(eye * column, axis=0, keepdims=True)
-        lin_ref[...] = jnp.sum(t * row - eye * now[2:3], axis=1, keepdims=True)
+        bh_ref[...], bl_ref[...] = found["b"]
+        lin_ref[...] = jnp.sum(t * found["row"] - eye * now[2:3], axis=1, keepdims=True)
 
     def stored_hess(k):
         product = dot3((th_ref[...], tl_ref[...]), (bh_ref[...], bl_ref[...]))
@@ -148,16 +163,16 @@
 
     def sweep(solve_first, solve):
         start()
-        phase(PHASES - 1, solve_first, term_ref[...])
+        phase(PHASES - 1, solve_first, True)
 
         def body(i, carry):
             k = PHASES - 1 - i
-            phase(k, solve, stored_hess(k + 1))
+            phase(k, solve, False)
             return carry
 
         lax.fori_loop(1, PHASES - section, body, 0)
 
-    sweep(lambda: quick(4), lambda: quick(3))
+    sweep(lambda side: quick(4, side), lambda side: quick(3, side))
 
     @pl.when(jnp.max(bad_ref[...]) > 0.0)
     def _():
@@ -173,14 +188,10 @@
     grad_ref[...] = turned[0:1, :height]
 
 
-def on_device(plant, actuation, state_weight, input_weight, state_grad, input_grad, defect, terminal_hess, terminal_grad):
-    height = N // lax.axis_size("inner")
-    zero = jnp.zeros((3, N), f32)
-    own = jnp.concatenate([state_weight, input_weight, state_grad, input_grad, defect, zero], axis=0)
-    copies = jnp.broadcast_to(own[None], (PHASES, 8, N))
-    gathered = lax.all_to_all(copies, "section", split_axis=0, concat_axis=0, tiled=True)
+def recursion(*arrays_and_height):
+    *arrays, height = arrays_and_height
     full = lambda dtype: pltpu.VMEM((N, N), dtype)
-    hess, grad = pl.pallas_call(
+    return pl.pallas_call(
         kernel,
         out_shape=(jax.ShapeDtypeStruct((height, N), f32), jax.ShapeDtypeStruct((1, height), f32)),
         in_specs=[pl.BlockSpec(memory_space=pltpu.VMEM)] * 5,
@@ -191,7 +202,16 @@
             full(bf16), full(bf16), full(bf16), full(bf16), full(bf16), full(bf16),
             full(f32), pltpu.VMEM((N, 1), f32), pltpu.VMEM((1, 1), f32), full(f32), full(f32),
         ],
-    )(gathered, plant, actuation, terminal_hess, terminal_grad[None])
+    )(*arrays)
+
+
+def on_device(plant, actuation, state_weight, input_weight, state_grad, input_grad, defect, terminal_hess, terminal_grad):
+    height = N // lax.axis_size("inner")
+    zero = jnp.zeros((3, N), f32)
+    own = jnp.concatenate([state_weight, input_weight, state_grad, input_grad, defect, zero], axis=0)
+    copies = jnp.broadcast_to(own[None], (PHASES, 8, N))
+    gathered = lax.all_to_all(copies, "section", split_axis=0, concat_axis=0, tiled=True)
+    hess, grad = recursion(gathered, plant, actuation, terminal_hess, terminal_grad[None], height)
     return hess[None], grad
 
 

time: 194 us -> 343 us (1.77)
  Pallas kernels: 174 us -> 324 us
    pallas_call x1, Pallas kernels: 174 us -> 324 us  [recursion(): pl.pallas_call(kernel, out_shape=(jax.ShapeDtypeStruct((height, N), f32),...]
where the time goes in v2:
time: 343 us
  Pallas kernels  324 us (94%)
  blocking collectives  17.1 us (5%)
    pallas_call x1, Pallas kernels, recursion(): pl.pallas_call(kernel, out_shape=(jax.ShapeDtypeStruct((height, N), f32),...  324 us
    all_to_all x1, blocking collectives, on_device(): lax.all_to_all(copies, 'section', split_axis=0, concat_axis=0, tiled=True)  17.1 us

profile of v2, /device:TPU:22, one launch (start us, length us, event | category | flops | bytes accessed | tf_op | source)
XLA Modules:
  0.0 343.2 jit_solution(2678775402655126418)
XLA Ops:
  0.6 0.0 copy-start.3
  0.6 0.0 copy-start.2
  0.7 0.0 copy-start.1
  0.7 0.0 copy-start
  0.7 0.6 copy-done.3
  1.3 0.0 copy-done.2
  1.3 0.0 copy-done.1
  1.3 0.0 copy-done
  1.4 0.7 concatenate.3
  2.1 17.1 %all_to_all.5.g_ref = f32[16,8,256]{2,1,0:T(8,128)} all-to-all(f32[16,8,256]{2,1,0:T(8,128)S(1)} %broadcast_in_dim.16), channel_id=1, replica_groups=mesh['section'=16,'inner'=16] {'section'}, dimensions={0} | all-to-all | bytes 262144 | tf_op jit(solution)/shard_map/all_to_all | solution.py:213
  19.2 324.0 %shard_map.104 = (f32[16,256]{1,0:T(8,128)}, f32[1,16]{1,0:T(1,128)}) custom-call(f32[16,8,256]{2,1,0:T(8,128)} %all_to_all.5.g_ref, f32[256,256]{1,0:T(8,128)} %plant_ref.1, f32[256,256]{1,0:T(8,128)} %act_ref.1, f32[256,256]{1,0:T(8,128)} %term_ref.1, f32[1,256]{1,0:T(1,128)} %bitcast.2), custom_call_target="tpu_custom_call" | custom-call | tf_op jit(solution)/shard_map/pallas_call | solution.py:194
  (2 shorter events, 0.0 us)
Async XLA Ops:
  0.6 0.7 copy-start.3
  0.6 0.7 copy-start.2
  0.7 0.7 copy-start.1
  0.7 0.7 copy-start

commit v3 on v2

v3 whole, which is shorter than its diff:
```python
import jax
import jax.numpy as jnp
from jax import lax
from jax.experimental import pallas as pl
from jax.experimental.pallas import tpu as pltpu
from jax.sharding import PartitionSpec as P

f32, bf16 = jnp.float32, jnp.bfloat16
N = 256
PHASES = 16
RUN = 5
highest = lax.Precision.HIGHEST


def split(x):
    head = x.astype(bf16)
    return head, (x - head.astype(f32)).astype(bf16)


def dot(a, b):
    return jnp.dot(a, b, preferred_element_type=f32)


def dot3(a, b):
    (ah, al), (bh, bl) = a, b
    return dot(jnp.concatenate([ah, ah, al], axis=1), jnp.concatenate([bh, bl, bh], axis=0))


def exact(a, b):
    return jnp.dot(a, b, precision=highest, preferred_element_type=f32)


def square_sum(x):
    return jnp.sum(jnp.sum(x * x, axis=0, keepdims=True), axis=1, keepdims=True)


def prepare(plant_ref, act_ref, ph_ref, plo_ref, pt_ref, pth_ref, ath_ref, atl_ref):
    plant = plant_ref[...]
    ph_ref[...], plo_ref[...] = split(plant)
    plant_t = plant.T
    pt_ref[...] = plant_t
    pth_ref[...] = plant_t.astype(bf16)
    ath_ref[...], atl_ref[...] = split(act_ref[...].T)


def kernel(
    g_ref, act_ref, term_ref, tgrad_ref, ph_ref, plo_ref, pt_ref, pth_ref, ath_ref, atl_ref, hess_ref, grad_ref,
    eye_ref, drift_ref,
    k_ref, kh_ref, kl_ref, hh_ref, hl_ref, sh_ref, sl_ref, s_ref, hess_all_ref, lin_all_ref, bad_ref, e_ref, x_ref,
):
    section = lax.axis_index("section")
    inner = lax.axis_index("inner")
    rows = lax.broadcasted_iota(jnp.int32, (N, N), 0)
    cols = lax.broadcasted_iota(jnp.int32, (N, N), 1)
    eye_ref[...] = jnp.where(rows == cols, 1.0, 0.0).astype(f32)
    drift_ref[...] = g_ref[:, 4, :] - exact(g_ref[:, 3, :] / g_ref[:, 1, :], ath_ref[...].astype(f32) + atl_ref[...].astype(f32))

    def start():
        hess = term_ref[...]
        hess_all_ref[PHASES] = hess
        hs = split(hess)
        hh_ref[...], hl_ref[...] = hs
        system = dot3(hs, split(spread(PHASES - 1)))
        k_ref[...] = system
        kh_ref[...], kl_ref[...] = split(system)
        s = spread(PHASES - 2)
        s_ref[...] = s
        sh_ref[...], sl_ref[...] = split(s)
        lin_all_ref[PHASES] = -jnp.sum(eye_ref[...] * tgrad_ref[...], axis=1, keepdims=True)
        bad_ref[...] = jnp.zeros((1, 1), f32)

    def quick(levels, beside):
        eye, pt = eye_ref[...], pt_ref[...]
        kh, kl = kh_ref[...], kl_ref[...]
        first = dot(jnp.concatenate([kh, pth_ref[...]], axis=0), kh)
        next(beside)
        k = k_ref[...]
        mu = jnp.sqrt(square_sum(k)) * 0.25
        al = 2.0 / (2.0 + mu)
        rho = mu * al * 0.5
        c = 2.0 / (2.0 - rho * rho)
        x = eye * (c * al * (2.0 - al)) - (c * al * al) * k
        t = (c * al * (2.0 - al)) * pt - (c * al * al) * first[N:]
        e = eye * (1.0 - c + c * (1.0 - al) * (1.0 - al)) - (2.0 * c * al * (1.0 - al)) * k
        e = e + (c * al * al) * first[:N]
        for _ in range(1, levels):
            rho = rho * rho / (2.0 - rho * rho)
            c = 2.0 / (2.0 - rho * rho)
            eh = e.astype(bf16)
            product = dot(jnp.concatenate([eh, x.astype(bf16), t.astype(bf16)], axis=0), eh)
            e = (1.0 - c) * eye + c * product[:N]
            x = c * (x + product[N : 2 * N])
            t = c * (t + product[2 * N :])
        next(beside)
        guess = t.astype(bf16)
        t = guess.astype(f32)
        residue = pt - t - dot(jnp.concatenate([guess, guess], axis=1), jnp.concatenate([kh, kl], axis=0))
        rho = rho * rho / (2.0 - rho * rho)
        c = 2.0 / (2.0 - rho * rho)
        eh = e.astype(bf16)
        product = dot(jnp.concatenate([x.astype(bf16), eh], axis=0), eh)
        x = c * (x + product[:N])
        e = (1.0 - c) * eye + c * product[N:]
        next(beside)
        t_new = t + dot(residue.astype(bf16), x.astype(bf16))
        left = square_sum(e)
        good = (left < 1e-2) & (left * square_sum(residue) < 1e-6 * square_sum(t))
        bad_ref[...] += jnp.where(good, 0.0, 1.0)
        next(beside)
        return t_new

    def careful(beside):
        for _ in range(4):
            next(beside)
        eye, pt = eye_ref[...], pt_ref[...]
        k = k_ref[...]
        most = jnp.max(jnp.sum(jnp.abs(k), axis=1, keepdims=True), axis=0, keepdims=True)
        mu = jnp.minimum(jnp.sqrt(square_sum(k)), most)
        al = 2.0 / (2.0 + mu)
        x_ref[...] = al * eye
        e_ref[...] = (1.0 - al) * eye - al * k

        def level(_, rho):
            c = 2.0 / (2.0 - rho * rho)
            e = e_ref[...]
            x_ref[...] = c * (x_ref[...] + exact(x_ref[...], e))
            e_ref[...] = (1.0 - c) * eye_ref[...] + c * exact(e, e)
            return rho * rho / (2.0 - rho * rho)

        lax.fori_loop(0, 24, level, mu * al * 0.5)
        e_ref[...] = exact(pt, x_ref[...])

        def refine(_, carry):
            k = k_ref[...]
            t = e_ref[...]
            e_ref[...] = t + exact(pt_ref[...] - t - exact(t, k), x_ref[...])
            return carry

        lax.fori_loop(0, 3, refine, 0)
        return e_ref[...]

    def spread(k):
        scaled = act_ref[...] / g_ref[jnp.maximum(k, 0)][1:2]
        return dot3(split(scaled), (ath_ref[...], atl_ref[...]))

    def phase(k, solve):
        now = g_ref[k]
        eye = eye_ref[...]
        found = {}

        def beside():
            found["b"] = split(dot3((hh_ref[...], hl_ref[...]), (ph_ref[...], plo_ref[...])))
            yield
            found["c"] = split(dot3(found["b"], (sh_ref[...], sl_ref[...])))
            yield
            product = hess_all_ref[k + 1] * drift_ref[pl.ds(k, 1), :]
            column = lin_all_ref[k + 1] - jnp.sum(product, axis=1, keepdims=True)
            found["row"] = jnp.sum(eye * column, axis=0, keepdims=True)
            found["weights"] = jnp.sum(eye * now[0:1], axis=1, keepdims=True)
            yield
            found["s"] = spread(k - 2)
            yield

        t = solve(beside())
        ts = split(t)
        system = dot3(ts, found["c"]) + found["weights"] * s_ref[...]
        k_ref[...] = system
        kh_ref[...], kl_ref[...] = split(system)
        hess = dot3(ts, found["b"]) + eye * now[0:1]
        hess_all_ref[k] = hess
        hh_ref[...], hl_ref[...] = split(hess)
        s_ref[...] = found["s"]
        sh_ref[...], sl_ref[...] = split(found["s"])
        lin_all_ref[k] = jnp.sum(t * found["row"] - eye * now[2:3], axis=1, keepdims=True)

    def sweep(solve_first, solve, run):
        start()
        phase(PHASES - 1, solve_first)

        def body(i, carry):
            for j in range(run):
                phase(PHASES - 2 - run * i - j, solve)
            return carry

        lax.fori_loop(0, (PHASES - 1) // run, body, 0)

    sweep(lambda side: quick(3, side), lambda side: quick(2, side), RUN)

    @pl.when(jnp.max(bad_ref[...]) > 0.0)
    def _():
        sweep(careful, careful, 1)

    height = hess_ref.shape[0]
    at = pl.multiple_of(inner * height, height)
    hess_ref[...] = hess_all_ref[section, pl.ds(at, height), :]
    row = jnp.sum(eye_ref[...] * lin_all_ref[section], axis=0, keepdims=True)
    turned = pltpu.roll(jnp.broadcast_to(-row, (8, N)), lax.rem(N - at, N), 1)
    grad_ref[...] = turned[0:1, :height]


def recursion(*arrays_and_height):
    *arrays, height = arrays_and_height
    full = lambda dtype: pltpu.VMEM((N, N), dtype)
    gathered, plant, actuation, terminal_hess, terminal_grad = arrays
    whole = pl.BlockSpec(memory_space=pltpu.VMEM)
    tables = pl.pallas_call(
        prepare,
        out_shape=tuple(jax.ShapeDtypeStruct((N, N), dtype) for dtype in (bf16, bf16, f32, bf16, bf16, bf16)),
        in_specs=[whole] * 2,
        out_specs=(whole,) * 6,
        cost_estimate=pl.CostEstimate(flops=1 << 20, bytes_accessed=1 << 21, transcendentals=0),
    )(plant, actuation)
    return pl.pallas_call(
        kernel,
        out_shape=(jax.ShapeDtypeStruct((height, N), f32), jax.ShapeDtypeStruct((1, height), f32)),
        in_specs=[whole] * 10,
        out_specs=(whole,) * 2,
        scratch_shapes=[
            full(f32), pltpu.VMEM((PHASES, N), f32),
            full(f32), full(bf16), full(bf16), full(bf16), full(bf16), full(bf16), full(bf16),
            full(f32), pltpu.VMEM((PHASES + 1, N, N), f32), pltpu.VMEM((PHASES + 1, N, 1), f32), pltpu.VMEM((1, 1), f32), full(f32), full(f32),
        ],
    )(gathered, actuation, terminal_hess, terminal_grad, *tables)


def on_device(plant, actuation, state_weight, input_weight, state_grad, input_grad, defect, terminal_hess, terminal_grad):
    height = N // lax.axis_size("inner")
    zero = jnp.zeros((3, N), f32)
    own = jnp.concatenate([state_weight, input_weight, state_grad, input_grad, defect, zero], axis=0)
    copies = jnp.broadcast_to(own[None], (PHASES, 8, N))
    gathered = lax.all_to_all(copies, "section", split_axis=0, concat_axis=0, tiled=True)
    hess, grad = recursion(gathered, plant, actuation, terminal_hess, terminal_grad[None], height)
    return hess[None], grad


def solution(mesh):
    data = P("section", None)
    in_specs = (P(), P(), data, data, data, data, data, P(), P())
    out_specs = (P("section", "inner", None), P("section", "inner"))
    return jax.shard_map(on_device, mesh=mesh, in_specs=in_specs, out_specs=out_specs, check_vma=False)
```

time: 343 us -> 340 us (level)
  blocking collectives: 17.1 us -> 0 us
  starting transfers between devices: 0 us -> 8.57 us
  waiting for transfers between devices: 0 us -> 6.65 us
  Pallas kernels: 324 us -> 319 us
    all_to_all x1 -> x0, blocking collectives: 17.1 us -> none  [on_device(): lax.all_to_all(copies, 'section', split_axis=0, concat_axis=0, tiled=True)]
    all_to_all x0 -> x1, starting transfers between devices: none -> 8.57 us  [on_device(): lax.all_to_all(copies, 'section', split_axis=0, concat_axis=0, tiled=True)]
    pallas_call x1, Pallas kernels: 324 us -> 317 us  [recursion(): pl.pallas_call(kernel, out_shape=(jax.ShapeDtypeStruct((height, N), f32),...]
    all_to_all x0 -> x1, waiting for transfers between devices: none -> 6.65 us  [on_device(): lax.all_to_all(copies, 'section', split_axis=0, concat_axis=0, tiled=True)]
  transfers between devices with their start and end apart: 0 -> 1, of which waited for: 0 -> 1; matrix products, arithmetic and copies ran while one was open for 0% -> 0% of each run, Pallas kernels for 0% -> 1%
where the time goes in v3:
time: 340 us; the launch traced here: 338 us
  Pallas kernels  319 us (94%)
  starting transfers between devices  8.57 us (3%)
  waiting for transfers between devices  6.65 us (2%)
    pallas_call x1, Pallas kernels, recursion(): pl.pallas_call(kernel, out_shape=(jax.ShapeDtypeStruct((height, N), f32),...  317 us
    all_to_all x1, starting transfers between devices, on_device(): lax.all_to_all(copies, 'section', split_axis=0, concat_axis=0, tiled=True)  8.57 us
  transfers between devices with their start and end apart: 1, of which 1 were waited for; matrix products, arithmetic and copies ran while one was open for 0% of the time, Pallas kernels for 1%

profile of v3, /device:TPU:22, one launch (start us, length us, event | category | flops | bytes accessed | tf_op | source)
XLA Modules:
  0.0 337.7 jit_solution(18066950672825176382)
XLA Ops:
  0.6 0.0 copy-start.4
  0.6 0.0 copy-start.3
  0.7 0.0 copy-start.2
  0.7 0.0 copy-start.1
  0.7 0.6 copy-done.4
  1.3 0.0 copy-done.3
  1.3 0.0 copy-done.2
  1.3 0.0 copy-done.1
  1.4 0.7 concatenate.3
  2.1 0.7 broadcast_in_dim.16
  2.7 8.6 %all-to-all-start = ((f32[16,8,256]{2,1,0:T(8,128)}), f32[16,8,256]{2,1,0:T(8,128)S(1)}, u32[]{:S(2)}, u32[]{:S(2)}) async-start(f32[16,8,256]{2,1,0:T(8,128)} %broadcast_in_dim.16), calls=%async_computation | async-start | bytes 262144 | tf_op jit(solution)/shard_map/all_to_all | solution.py:231
  11.3 2.0 shard_map.104
  13.3 6.6 %all-to-all-done.g_ref = f32[16,8,256]{2,1,0:T(8,128)S(1)} async-done(((f32[16,8,256]{2,1,0:T(8,128)}), f32[16,8,256]{2,1,0:T(8,128)S(1)}, u32[]{:S(2)}, u32[]{:S(2)}) %all-to-all-start) | async-done | bytes 131104 | tf_op jit(solution)/shard_map/all_to_all | solution.py:231
  19.9 0.0 copy-start
  20.0 0.6 copy-done
  20.6 317.1 %shard_map.105 = (f32[16,256]{1,0:T(8,128)}, f32[1,16]{1,0:T(1,128)}) custom-call(f32[16,8,256]{2,1,0:T(8,128)} %copy-done, f32[256,256]{1,0:T(8,128)} %act_ref.3, f32[256,256]{1,0:T(8,128)} %term_ref.1, f32[1,256]{1,0:T(1,128)} %bitcast.2, bf16[256,256]{1,0:T(8,128)(2,1)} %get-tuple-element.10.ph_ref, bf16[256,256]{1,0:T(8,128)(2,1)} %get-tuple-element.11.plo_ref, ...), custom_call_target="tpu_custom_call" | custom-call | tf_op jit(solution)/shard_map/pallas_call | solution.py:213
  (1 shorter events, 0.0 us)
Async XLA Ops:
  0.6 0.7 copy-start.4
  0.6 0.7 copy-start.3
  0.7 0.7 copy-start.2
  0.7 0.7 copy-start.1
  2.7 17.2 %all-to-all-start = ((f32[16,8,256]{2,1,0:T(8,128)}), f32[16,8,256]{2,1,0:T(8,128)S(1)}, u32[]{:S(2)}, u32[]{:S(2)}) async-start(f32[16,8,256]{2,1,0:T(8,128)} %broadcast_in_dim.16), calls=%async_computation | async-start | bytes 262144 | tf_op jit(solution)/shard_map/all_to_all | solution.py:231
  19.9 0.7 copy-start

commit v4 on v3

--- a/solution.py
+++ b/solution.py
@@ -34,26 +34,25 @@
     return jnp.sum(jnp.sum(x * x, axis=0, keepdims=True), axis=1, keepdims=True)
 
 
-def prepare(plant_ref, act_ref, ph_ref, plo_ref, pt_ref, pth_ref, ath_ref, atl_ref):
+def kernel(
+    g_ref, plant_ref, act_ref, term_ref, tgrad_ref, hess_ref, grad_ref,
+    ph_ref, plo_ref, pt_ref, pth_ref, ath_ref, atl_ref, eye_ref, drift_ref,
+    k_ref, kh_ref, kl_ref, hh_ref, hl_ref, sh_ref, sl_ref, s_ref, hess_all_ref, lin_all_ref, bad_ref, e_ref, x_ref,
+):
+    section = lax.axis_index("section")
+    inner = lax.axis_index("inner")
     plant = plant_ref[...]
+    act = act_ref[...]
     ph_ref[...], plo_ref[...] = split(plant)
     plant_t = plant.T
     pt_ref[...] = plant_t
     pth_ref[...] = plant_t.astype(bf16)
-    ath_ref[...], atl_ref[...] = split(act_ref[...].T)
-
-
-def kernel(
-    g_ref, act_ref, term_ref, tgrad_ref, ph_ref, plo_ref, pt_ref, pth_ref, ath_ref, atl_ref, hess_ref, grad_ref,
-    eye_ref, drift_ref,
-    k_ref, kh_ref, kl_ref, hh_ref, hl_ref, sh_ref, sl_ref, s_ref, hess_all_ref, lin_all_ref, bad_ref, e_ref, x_ref,
-):
-    section = lax.axis_index("section")
-    inner = lax.axis_index("inner")
+    act_t = act.T
+    ath_ref[...], atl_ref[...] = split(act_t)
     rows = lax.broadcasted_iota(jnp.int32, (N, N), 0)
     cols = lax.broadcasted_iota(jnp.int32, (N, N), 1)
     eye_ref[...] = jnp.where(rows == cols, 1.0, 0.0).astype(f32)
-    drift_ref[...] = g_ref[:, 4, :] - exact(g_ref[:, 3, :] / g_ref[:, 1, :], ath_ref[...].astype(f32) + atl_ref[...].astype(f32))
+    drift_ref[...] = g_ref[:, 4, :] - exact(g_ref[:, 3, :] / g_ref[:, 1, :], act_t)
 
     def start():
         hess = term_ref[...]
@@ -201,26 +200,18 @@
 def recursion(*arrays_and_height):
     *arrays, height = arrays_and_height
     full = lambda dtype: pltpu.VMEM((N, N), dtype)
-    gathered, plant, actuation, terminal_hess, terminal_grad = arrays
-    whole = pl.BlockSpec(memory_space=pltpu.VMEM)
-    tables = pl.pallas_call(
-        prepare,
-        out_shape=tuple(jax.ShapeDtypeStruct((N, N), dtype) for dtype in (bf16, bf16, f32, bf16, bf16, bf16)),
-        in_specs=[whole] * 2,
-        out_specs=(whole,) * 6,
-        cost_estimate=pl.CostEstimate(flops=1 << 20, bytes_accessed=1 << 21, transcendentals=0),
-    )(plant, actuation)
     return pl.pallas_call(
         kernel,
         out_shape=(jax.ShapeDtypeStruct((height, N), f32), jax.ShapeDtypeStruct((1, height), f32)),
-        in_specs=[whole] * 10,
-        out_specs=(whole,) * 2,
+        in_specs=[pl.BlockSpec(memory_space=pltpu.VMEM)] * 5,
+        out_specs=(pl.BlockSpec(memory_space=pltpu.VMEM),) * 2,
         scratch_shapes=[
+            full(bf16), full(bf16), full(f32), full(bf16), full(bf16), full(bf16),
             full(f32), pltpu.VMEM((PHASES, N), f32),
             full(f32), full(bf16), full(bf16), full(bf16), full(bf16), full(bf16), full(bf16),
             full(f32), pltpu.VMEM((PHASES + 1, N, N), f32), pltpu.VMEM((PHASES + 1, N, 1), f32), pltpu.VMEM((1, 1), f32), full(f32), full(f32),
         ],
-    )(gathered, actuation, terminal_hess, terminal_grad, *tables)
+    )(*arrays)
 
 
 def on_device(plant, actuation, state_weight, input_weight, state_grad, input_grad, defect, terminal_hess, terminal_grad):

time: 340 us -> 338 us (level)
  blocking collectives: 0 us -> 17.1 us
  starting transfers between devices: 8.57 us -> 0 us
  waiting for transfers between devices: 6.65 us -> 0 us
    all_to_all x0 -> x1, blocking collectives: none -> 17.1 us  [on_device(): lax.all_to_all(copies, 'section', split_axis=0, concat_axis=0, tiled=True)]
    all_to_all x1 -> x0, starting transfers between devices: 8.57 us -> none  [on_device(): lax.all_to_all(copies, 'section', split_axis=0, concat_axis=0, tiled=True)]
    all_to_all x1 -> x0, waiting for transfers between devices: 6.65 us -> none  [on_device(): lax.all_to_all(copies, 'section', split_axis=0, concat_axis=0, tiled=True)]
  transfers between devices with their start and end apart: 1 -> 0, of which waited for: 1 -> 0; matrix products, arithmetic and copies ran while one was open for 0% -> 0% of each run, Pallas kernels for 1% -> 0%
where the time goes in v4:
time: 338 us; the launch traced here: 336 us
  Pallas kernels  317 us (94%)
  blocking collectives  17.1 us (5%)
    pallas_call x1, Pallas kernels, recursion(): pl.pallas_call(kernel, out_shape=(jax.ShapeDtypeStruct((height, N), f32),...  317 us
    all_to_all x1, blocking collectives, on_device(): lax.all_to_all(copies, 'section', split_axis=0, concat_axis=0, tiled=True)  17.1 us

profile of v4, /device:TPU:22, one launch (start us, length us, event | category | flops | bytes accessed | tf_op | source)
XLA Modules:
  0.0 336.1 jit_solution(16164817841360265071)
XLA Ops:
  0.6 0.0 copy-start.3
  0.6 0.0 copy-start.2
  0.7 0.0 copy-start.1
  0.7 0.0 copy-start
  0.7 0.6 copy-done.3
  1.3 0.0 copy-done.2
  1.3 0.0 copy-done.1
  1.3 0.0 copy-done
  1.4 0.7 concatenate.3
  2.1 17.1 %all_to_all.5.g_ref = f32[16,8,256]{2,1,0:T(8,128)} all-to-all(f32[16,8,256]{2,1,0:T(8,128)S(1)} %broadcast_in_dim.16), channel_id=1, replica_groups=mesh['section'=16,'inner'=16] {'section'}, dimensions={0} | all-to-all | bytes 262144 | tf_op jit(solution)/shard_map/all_to_all | solution.py:222
  19.2 316.9 %shard_map.104 = (f32[16,256]{1,0:T(8,128)}, f32[1,16]{1,0:T(1,128)}) custom-call(f32[16,8,256]{2,1,0:T(8,128)} %all_to_all.5.g_ref, f32[256,256]{1,0:T(8,128)} %plant_ref.1, f32[256,256]{1,0:T(8,128)} %act_ref.1, f32[256,256]{1,0:T(8,128)} %term_ref.1, f32[1,256]{1,0:T(1,128)} %bitcast.2), custom_call_target="tpu_custom_call" | custom-call | tf_op jit(solution)/shard_map/pallas_call | solution.py:203
  (2 shorter events, 0.0 us)
Async XLA Ops:
  0.6 0.7 copy-start.3
  0.6 0.7 copy-start.2
  0.7 0.7 copy-start.1
  0.7 0.7 copy-start

commit v5 on v4

--- a/solution.py
+++ b/solution.py
@@ -86,10 +86,10 @@
             rho = rho * rho / (2.0 - rho * rho)
             c = 2.0 / (2.0 - rho * rho)
             eh = e.astype(bf16)
-            product = dot(jnp.concatenate([eh, x.astype(bf16), t.astype(bf16)], axis=0), eh)
-            e = (1.0 - c) * eye + c * product[:N]
-            x = c * (x + product[N : 2 * N])
-            t = c * (t + product[2 * N :])
+            product = dot(jnp.concatenate([t.astype(bf16), eh, x.astype(bf16)], axis=0), eh)
+            t = c * (t + product[:N])
+            e = (1.0 - c) * eye + c * product[N : 2 * N]
+            x = c * (x + product[2 * N :])
         next(beside)
         guess = t.astype(bf16)
         t = guess.astype(f32)

time: 338 us -> 337 us (level)
  no operation moved by 1% of the time
where the time goes in v5:
time: 337 us; the launch traced here: 335 us
  Pallas kernels  316 us (94%)
  blocking collectives  17.1 us (5%)
    pallas_call x1, Pallas kernels, recursion(): pl.pallas_call(kernel, out_shape=(jax.ShapeDtypeStruct((height, N), f32),...  316 us
    all_to_all x1, blocking collectives, on_device(): lax.all_to_all(copies, 'section', split_axis=0, concat_axis=0, tiled=True)  17.1 us

profile of v5, /device:TPU:22, one launch (start us, length us, event | category | flops | bytes accessed | tf_op | source)
XLA Modules:
  0.0 335.3 jit_solution(3380924840660160353)
XLA Ops:
  0.6 0.0 copy-start.3
  0.6 0.0 copy-start.2
  0.7 0.0 copy-start.1
  0.7 0.0 copy-start
  0.7 0.6 copy-done.3
  1.3 0.0 copy-done.2
  1.3 0.0 copy-done.1
  1.3 0.0 copy-done
  1.4 0.7 concatenate.3
  2.1 17.1 %all_to_all.5.g_ref = f32[16,8,256]{2,1,0:T(8,128)} all-to-all(f32[16,8,256]{2,1,0:T(8,128)S(1)} %broadcast_in_dim.16), channel_id=1, replica_groups=mesh['section'=16,'inner'=16] {'section'}, dimensions={0} | all-to-all | bytes 262144 | tf_op jit(solution)/shard_map/all_to_all | solution.py:222
  19.2 316.1 %shard_map.104 = (f32[16,256]{1,0:T(8,128)}, f32[1,16]{1,0:T(1,128)}) custom-call(f32[16,8,256]{2,1,0:T(8,128)} %all_to_all.5.g_ref, f32[256,256]{1,0:T(8,128)} %plant_ref.1, f32[256,256]{1,0:T(8,128)} %act_ref.1, f32[256,256]{1,0:T(8,128)} %term_ref.1, f32[1,256]{1,0:T(1,128)} %bitcast.2), custom_call_target="tpu_custom_call" | custom-call | tf_op jit(solution)/shard_map/pallas_call | solution.py:203
  (2 shorter events, 0.0 us)
Async XLA Ops:
  0.6 0.7 copy-start.3
  0.6 0.7 copy-start.2
  0.7 0.7 copy-start.1
  0.7 0.7 copy-start
